TPU v7x, 512 devices: a whole 4x8x8 slice. The times are simulated.
512 devices in a mesh: gx: 8 (over x, core), gy: 8 (over z), gz: 8 (over y).
Axes of the slice: x: 4, y: 8, z: 8, core: 2. Of those that a mesh axis runs over, the one named last changes fastest.
Arguments:
- features: float32 [32, 262144], P(None, ('gx', 'gy', 'gz')), may hold values from -6 to 6
- edge_lists: int32 [2, 1048576], P(None, ('gx', 'gy', 'gz')), may hold values from 0 to 512, as said below
- peer_nodes: int32 [27, 16384], P(None, ('gx', 'gy', 'gz')), may hold values from 0 to 512, as said below
- edge_in: float32 [2, 32, 64], replicated, may hold values from -0.75 to 0.75
- edge_out: float32 [2, 32, 32], replicated, may hold values from -1 to 1
- node_in: float32 [2, 32, 64], replicated, may hold values from -0.75 to 0.75
- node_out: float32 [2, 32, 32], replicated, may hold values from -1 to 1
- cotangent: float32 [32, 262144], P(None, ('gx', 'gy', 'gz')), may hold values from -6 to 6
Outputs:
- updated: float32 [32, 262144], P(None, ('gx', 'gy', 'gz'))
- feature_grad: float32 [32, 262144], P(None, ('gx', 'gy', 'gz'))
Inputs may be any that keep to these rules, and one draw needn't show every extreme that they name: `edge_lists`: row 0 holds sources and row 1 targets. 512 marks an empty edge in both rows; each device's live edges come first, from two fifths of its 2048 slots to all of them, and some device has all live. `peer_nodes`: row k of a device's block lists its nodes coincident with nodes of the device at grid offset (k // 9 - 1, k // 3 % 3 - 1, k % 3 - 1); 512 marks an empty slot and filled slots come first. Slot s of row k and slot s of that neighbour's row 26 - k are filled together and name the same coincident node. No index repeats within a device's block. Row 13 and rows toward devices outside the grid are empty. Rows toward face neighbours fill 32 // 4 to 32 slots, and some pair fills 32; rows toward edge and corner neighbours fill at most 4 slots, and some pair fills 4.
All inputs are finite; a program needn't handle non-finite values.
Results may differ from a plain program's by a relative error of at most 0.0001.
Values sent between devices are 32-bit elements; how exact they have to be, the bound alone decides.
A program may use at most 64 MiB of HBM per device.

v0:
```python
import functools

import jax
import jax.numpy as jnp
from jax import lax
from jax.experimental import pallas as pl
from jax.experimental.pallas import tpu as pltpu
from jax.sharding import PartitionSpec as P

F = 32
LANES = 128
AXES = ("gx", "gy", "gz")
LINKS = [(k // 9 - 1, k // 3 % 3 - 1, k % 3 - 1) for k in range(27)]
REACH = [sum(abs(c) for c in offset) for offset in LINKS]
FACES = [k for k in range(27) if REACH[k] == 1]
RIMS = [k for k in range(27) if REACH[k] > 1]
ORDER = sorted(RIMS, key=lambda k: -REACH[k]) + FACES
RIM_ROW = 8 * len(FACES)
ROWS = 80
f32, bf16, i32 = jnp.float32, jnp.bfloat16, jnp.int32


def split(value):
    high = value.astype(bf16)
    low = (value - high.astype(f32)).astype(bf16)
    return high, low


def dot(left, right):
    return lax.dot_general(left, right, (((1,), (0,)), ((), ())), preferred_element_type=f32)


def spread(matrix):
    rows = matrix.shape[0]
    wide = jnp.concatenate([matrix] * (LANES // matrix.shape[1]), axis=1)
    high, low = split(0.5 * wide)
    return jnp.where(iota((rows, LANES), 1) < LANES // 2, high.astype(f32), low.astype(f32)).astype(bf16)


def spread_flipped(matrix):
    rows = matrix.shape[0]
    tall = jnp.concatenate([matrix] * (LANES // rows), axis=0)
    wide = jnp.transpose(jnp.concatenate([tall, jnp.zeros((LANES, LANES - F), f32)], axis=1))[:F]
    high, low = split(0.5 * wide)
    if rows == 64:
        return jnp.concatenate([high, low], axis=1)
    return jnp.where(iota((F, LANES), 1) < LANES // 2, high.astype(f32), low.astype(f32)).astype(bf16)


def times(weights, value):
    high, low = split(value)
    return 2.0 * dot(weights, jnp.concatenate([high, low, high, low], axis=0))


def sigmoid_of(value):
    return 0.5 * jnp.tanh(0.5 * value) + 0.5


def lane_take(chunk, index):
    return jnp.take_along_axis(chunk, index, axis=1, mode="promise_in_bounds")


def iota(shape, dim):
    return lax.broadcasted_iota(i32, shape, dim)


def take(table, index):
    rows = table.shape[0]
    index = jnp.broadcast_to(index, (8, LANES))
    lane, part = index & (LANES - 1), index >> 7
    pieces = []
    for top in range(0, rows, 8):
        total = jnp.zeros((8, LANES), f32)
        for chunk in range(table.shape[1] // LANES):
            got = lane_take(table[top : top + 8, chunk * LANES : (chunk + 1) * LANES], lane)
            total = jnp.where(part == chunk, got, total)
        pieces.append(total)
    return jnp.concatenate(pieces, axis=0)


def kernel(
    sizes, x_ref, edges_ref, peers_ref, edge_in_ref, edge_out_ref, node_in_ref, node_out_ref, cot_ref,
    updated_ref, grad_ref,
    hot_target, hot_source, slopes, masked, peer_pad, held,
    face_out, rim_out, face_in, rim_in, send_sem, recv_sem,
):
    here = [lax.axis_index(axis) for axis in AXES]
    nodes = x_ref.shape[1]
    edges = edges_ref.shape[1]
    blocks = edges // LANES
    chunks = nodes // LANES

    def there(k):
        inside = True
        for place, step, size in zip(here, LINKS[k], sizes):
            if step < 0:
                inside = inside & (place > 0)
            elif step > 0:
                inside = inside & (place < size - 1)
        return inside

    def device(k):
        return tuple(place + step for place, step in zip(here, LINKS[k]))

    def copy(turn, k):
        if REACH[k] == 1:
            source = face_out.at[turn, FACES.index(k)]
            target = face_in.at[turn, FACES.index(26 - k)]
        else:
            source = rim_out.at[turn, k]
            target = rim_in.at[turn, 26 - k]
        return pltpu.make_async_remote_copy(
            src_ref=source, dst_ref=target, send_sem=send_sem.at[turn, k], recv_sem=recv_sem.at[turn, 26 - k],
            device_id=device(k), device_id_type=pl.DeviceIdType.MESH,
        )

    barrier = pltpu.get_barrier_semaphore()
    present = jnp.int32(0)
    for k in ORDER:
        present = present + jnp.where(there(k), 1, 0).astype(i32)

        @pl.when(there(k))
        def _():
            pl.semaphore_signal(barrier, inc=1, device_id=device(k), device_id_type=pl.DeviceIdType.MESH)

    def source_of(block):
        return edges_ref[0:1, block * LANES : (block + 1) * LANES]

    def target_of(block):
        return edges_ref[1:2, block * LANES : (block + 1) * LANES]

    def build_hot(hot, index_of):
        row = iota((256, LANES), 0)
        for block in range(blocks):
            index = jnp.broadcast_to(index_of(block) & 255, (256, LANES))
            hot[:, block * LANES : (block + 1) * LANES] = jnp.where(row == index, 1.0, 0.0).astype(bf16)

    peer_pad[...] = jnp.full(peer_pad.shape, 512, i32)
    peer_pad[0:27, 0 : peers_ref.shape[1]] = peers_ref[...]
    lane = iota((8, LANES), 1)
    group = iota((8, LANES), 0)
    by_slot = jnp.transpose(peer_pad[...].astype(f32)).astype(i32)[0:8]
    rim_index = lane - RIM_ROW
    slot_node = lane_take(by_slot, jnp.maximum(rim_index, 0))
    keep = jnp.zeros((8, LANES), jnp.bool_)
    for k in RIMS:
        keep = keep | (rim_index == k)
    slot_node = jnp.where(keep & (group < 4), slot_node, 512)
    for p, k in enumerate(FACES):
        row = jnp.broadcast_to(peer_pad[k : k + 1, :], (8, LANES))
        got = lane_take(row, 8 * group + (lane & 7))
        slot_node = jnp.where(lane >> 3 == p, got, slot_node)

    def node_slots():
        padded = jnp.concatenate([slot_node, jnp.full((LANES - 8, LANES), 512, i32)], axis=0)
        by_row = jnp.transpose(padded.astype(f32)).astype(i32)[0:ROWS]
        rows = iota((ROWS, LANES), 0)
        codes = []
        for chunk in range(chunks):
            node = iota((ROWS, LANES), 1) + chunk * LANES
            code = jnp.zeros((ROWS, LANES), f32)
            for g in range(4):
                column = jnp.broadcast_to(by_row[:, g : g + 1], (ROWS, LANES))
                code = code + jnp.where(column == node, rows + (LANES * g + 1), 0).astype(f32)
            codes.append(jnp.sum(code, axis=0, keepdims=True).astype(i32))
        return codes

    def pack(turn, field):
        columns = [take(field, slot_node[g : g + 1]) for g in range(4)]
        packed = jnp.transpose(jnp.concatenate(columns, axis=0))
        for p in range(len(FACES)):
            face_out[turn, p] = packed[8 * p : 8 * p + 8]
        for k in RIMS:
            rim_out[turn, k] = packed[RIM_ROW + k : RIM_ROW + k + 1]

    def send(turn):
        for k in ORDER:

            @pl.when(there(k))
            def _():
                copy(turn, k).start()

    def receive(turn):
        for k in FACES + RIMS[::-1]:

            @pl.when(there(k))
            def _():
                copy(turn, 26 - k).wait_recv()

    def unpack(turn, codes):
        faces = face_in[turn].reshape(RIM_ROW, LANES)
        rims = rim_in[turn].reshape(rim_in.shape[1], LANES)
        arrived = jnp.concatenate([faces, rims], axis=0)
        arrived = jnp.concatenate([arrived, jnp.zeros((LANES - arrived.shape[0], LANES), f32)], axis=0)
        columns = jnp.transpose(arrived)
        pieces = []
        for chunk in range(chunks):
            code = jnp.broadcast_to(codes[chunk] - 1, (8, LANES))
            row, which = code & (LANES - 1), code >> 7
            tops = []
            for top in range(0, F, 8):
                total = jnp.zeros((8, LANES), f32)
                for g in range(4):
                    got = lane_take(columns[F * g + top : F * g + top + 8], row)
                    total = jnp.where(which == g, got, total)
                tops.append(total)
            pieces.append(jnp.concatenate(tops, axis=0))
        return jnp.concatenate(pieces, axis=1)

    def put_masked(block, value, index):
        half = jnp.broadcast_to(index >> 8, (F, LANES))
        columns = slice(block * LANES, (block + 1) * LANES)
        for part in range(2):
            high, low = split(jnp.where(half == part, value, 0.0))
            masked[64 * part : 64 * part + 32, columns] = high
            masked[64 * part + 32 : 64 * part + 64, columns] = low

    def scatter(hot):
        total = lax.dot_general(
            masked[...], hot[...], (((1,), (1,)), ((), ())), preferred_element_type=f32
        )
        return jnp.concatenate([total[0:32] + total[32:64], total[64:96] + total[96:128]], axis=1)

    def edge_forward(layer, table):
        first, second = table[:F], table[F:]
        for block in range(blocks):
            pre = take(first, source_of(block)) + take(second, target_of(block))
            gate = sigmoid_of(pre)
            slopes[layer, :, block * LANES : (block + 1) * LANES] = gate * (1.0 + pre * (1.0 - gate))
            put_masked(block, pre * gate, target_of(block))
        return scatter(hot_target)

    def edge_backward(layer, table):
        deltas = []
        for block in range(blocks):
            delta = take(table, target_of(block)) * slopes[layer, :, block * LANES : (block + 1) * LANES]
            deltas.append(delta)
            put_masked(block, delta, target_of(block))
        to_target = scatter(hot_target)
        for block in range(blocks):
            put_masked(block, deltas[block], source_of(block))
        to_source = scatter(hot_source)
        return jnp.concatenate([to_source, to_target], axis=0)

    ends, joint, own, out, mixed = [], [], [], [], []
    for layer in range(2):
        entry = edge_in_ref[layer]
        node = node_in_ref[layer]
        ends.append(jnp.concatenate([entry[:, :F], entry[:, F:]], axis=0))
        own.append(node[:, :F])
        out.append(node_out_ref[layer])
        wide = jnp.concatenate([edge_out_ref[layer]] * 4, axis=1)
        mixed.append(times(spread(node[:, F:]), wide)[:, :F])

    field = x_ref[...]
    build_hot(hot_target, target_of)
    sums = edge_forward(0, times(spread(ends[0]), field))
    pack(0, sums)
    pl.semaphore_wait(barrier, present)
    send(0)

    codes = node_slots()
    build_hot(hot_source, source_of)
    held[0] = times(spread(own[0]), field)
    receive(0)
    pre = held[0] + times(spread(mixed[0]), sums + unpack(0, codes))
    gate = sigmoid_of(pre)
    node_slope = gate * (1.0 + pre * (1.0 - gate))
    field = field + times(spread(out[0]), pre * gate)

    sums = edge_forward(1, times(spread(ends[1]), field))
    pack(1, sums)
    send(1)
    held[1] = times(spread(own[1]), field)
    cot = cot_ref[...]
    lifted = times(spread_flipped(out[1]), cot)
    receive(1)
    pre = held[1] + times(spread(mixed[1]), sums + unpack(1, codes))
    gate = sigmoid_of(pre)

    delta = lifted * (gate * (1.0 + pre * (1.0 - gate)))
    sums = times(spread_flipped(mixed[1]), delta)
    pack(2, sums)
    send(2)
    updated_ref[...] = field + times(spread(out[1]), pre * gate)
    held[2] = cot + times(spread_flipped(own[1]), delta)
    receive(2)
    both = edge_backward(1, sums + unpack(2, codes))
    upstream = held[2] + times(spread_flipped(ends[1]), both)
    delta = times(spread_flipped(out[0]), upstream) * node_slope
    sums = times(spread_flipped(mixed[0]), delta)
    pack(3, sums)
    send(3)
    held[3] = upstream + times(spread_flipped(own[0]), delta)
    receive(3)
    both = edge_backward(0, sums + unpack(3, codes))
    grad_ref[...] = held[3] + times(spread_flipped(ends[0]), both)

    for turn in range(4):
        for k in ORDER:

            @pl.when(there(k))
            def _():
                copy(turn, k).wait_send()


def solution(mesh):
    sizes = tuple(mesh.shape[axis] for axis in AXES)

    def on_device(features, edge_lists, peer_nodes, edge_in, edge_out, node_in, node_out, cotangent):
        nodes = features.shape[1]
        edges = edge_lists.shape[1]
        vmem = pl.BlockSpec(memory_space=pltpu.VMEM)
        return pl.pallas_call(
            functools.partial(kernel, sizes),
            out_shape=(jax.ShapeDtypeStruct(features.shape, f32), jax.ShapeDtypeStruct(features.shape, f32)),
            in_specs=[vmem] * 8,
            out_specs=(vmem, vmem),
            scratch_shapes=[
                pltpu.VMEM((256, edges), bf16),
                pltpu.VMEM((256, edges), bf16),
                pltpu.VMEM((2, F, edges), f32),
                pltpu.VMEM((128, edges), bf16),
                pltpu.VMEM((LANES, LANES), i32),
                pltpu.VMEM((4, F, nodes), f32),
                pltpu.VMEM((4, len(FACES), 8, LANES), f32),
                pltpu.VMEM((4, 27, 1, LANES), f32),
                pltpu.VMEM((4, len(FACES), 8, LANES), f32),
                pltpu.VMEM((4, 27, 1, LANES), f32),
                pltpu.SemaphoreType.DMA((4, 27)),
                pltpu.SemaphoreType.DMA((4, 27)),
            ],
            compiler_params=pltpu.CompilerParams(collective_id=0, has_side_effects=True),
        )(features, edge_lists, peer_nodes, edge_in, edge_out, node_in, node_out, cotangent)

    split_columns = P(None, AXES)
    return jax.shard_map(
        on_device,
        mesh=mesh,
        in_specs=(split_columns, split_columns, split_columns, P(), P(), P(), P(), split_columns),
        out_specs=(split_columns, split_columns),
        check_vma=False,
    )
```

profile of v0, /device:TPU:1, one launch (start us, length us, event | category | flops | bytes accessed | tf_op | source)
XLA Modules:
  0.0 40.1 jit_solution(11154681226259379948)
XLA Ops:
  0.6 37.3 %shard_map.95 = (f32[32,512]{1,0:T(8,128)}, f32[32,512]{1,0:T(8,128)}) custom-call(f32[32,512]{1,0:T(8,128)} %x_ref.1, s32[2,2048]{1,0:T(2,128)} %edges_ref.1, s32[27,32]{1,0:T(8,128)} %peers_ref.1, f32[2,32,64]{2,1,0:T(8,128)} %edge_in_ref.1, f32[2,32,32]{2,1,0:T(8,128)} %edge_out_ref.1, f32[2,32,64]{2,1,0:T(8,128)} %node_in_ref.1, ...), custom_call_target="tpu_custom_call" | custom-call | tf_op jit(solution)/shard_map/pallas_call | solution.py:314
  38.0 0.0 copy-start
  38.0 1.5 %copy.12 = f32[32,512]{1,0:T(8,128)} copy(f32[32,512]{1,0:T(8,128)} %get-tuple-element.4) | data formatting | bytes 131072
  39.5 0.0 copy-done
  39.5 0.6 %copy.13 = f32[32,512]{1,0:T(8,128)} copy(f32[32,512]{1,0:T(8,128)S(1)} %copy-done) | data formatting | bytes 131072
Async XLA Ops:
  38.0 1.5 %copy-start = (f32[32,512]{1,0:T(8,128)S(1)}, f32[32,512]{1,0:T(8,128)}, u32[]{:S(2)}) copy-start(f32[32,512]{1,0:T(8,128)} %get-tuple-element.5) | copy-start | bytes 196612
where the time goes:
time: 40.5 us; the launch traced here: 40.1 us
  Pallas kernels  37.3 us (92%)
  local copies, waits for them, and re-layouts  2.14 us (5%)
  between operations  0.65 us (2%)
    pallas_call x1, Pallas kernels, on_device(): pl.pallas_call(functools.partial(kernel, sizes), out_shape=(jax.ShapeDtyp...  37.3 us
    unnamed x4, local copies, waits for them, and re-layouts  2.14 us

commit v1 on v0

--- a/solution.py
+++ b/solution.py
@@ -79,9 +79,10 @@
 
 
 def kernel(
-    sizes, x_ref, edges_ref, peers_ref, edge_in_ref, edge_out_ref, node_in_ref, node_out_ref, cot_ref,
+    sizes, x_hbm, edges_hbm, peers_hbm, edge_in_hbm, edge_out_hbm, node_in_hbm, node_out_hbm, cot_hbm,
     updated_ref, grad_ref,
-    hot_target, hot_source, slopes, masked, peer_pad, held,
+    x_ref, edges_ref, peers_ref, edge_in_ref, edge_out_ref, node_in_ref, node_out_ref, cot_ref, load_sem,
+    hot_target, hot_source, slopes, masked, peer_pad, held, ends_to, small_to, ends_from,
     face_out, rim_out, face_in, rim_in, send_sem, recv_sem,
 ):
     here = [lax.axis_index(axis) for axis in AXES]
@@ -91,12 +92,11 @@
     chunks = nodes // LANES
 
     def there(k):
-        inside = True
+        inside = None
         for place, step, size in zip(here, LINKS[k], sizes):
-            if step < 0:
-                inside = inside & (place > 0)
-            elif step > 0:
-                inside = inside & (place < size - 1)
+            if step:
+                ok = place > 0 if step < 0 else place < size - 1
+                inside = ok if inside is None else inside & ok
         return inside
 
     def device(k):
@@ -110,18 +110,37 @@
             source = rim_out.at[turn, k]
             target = rim_in.at[turn, 26 - k]
         return pltpu.make_async_remote_copy(
-            src_ref=source, dst_ref=target, send_sem=send_sem.at[turn, k], recv_sem=recv_sem.at[turn, 26 - k],
+            src_ref=source, dst_ref=target,
+            send_sem=send_sem.at[min(REACH[k], 2) - 1], recv_sem=recv_sem.at[turn, min(REACH[k], 2) - 1],
             device_id=device(k), device_id_type=pl.DeviceIdType.MESH,
         )
 
+    at_rim = jnp.int32(0)
+    for place, size in zip(here, sizes):
+        at_rim = at_rim + jnp.where((place == 0) | (place == size - 1), 1, 0).astype(i32)
+    counts = [(6 - rim, 3 ** (3 - rim) * 2**rim - 7 + rim) for rim in range(4)]
+
     barrier = pltpu.get_barrier_semaphore()
-    present = jnp.int32(0)
     for k in ORDER:
-        present = present + jnp.where(there(k), 1, 0).astype(i32)
 
         @pl.when(there(k))
         def _():
             pl.semaphore_signal(barrier, inc=1, device_id=device(k), device_id_type=pl.DeviceIdType.MESH)
+
+    loads = [
+        pltpu.make_async_copy(source, target, load_sem.at[at])
+        for at, (source, target) in enumerate(
+            (
+                (x_hbm, x_ref), (edge_in_hbm, edge_in_ref), (edges_hbm, edges_ref), (peers_hbm, peers_ref),
+                (edge_out_hbm, edge_out_ref), (node_in_hbm, node_in_ref), (node_out_hbm, node_out_ref),
+                (cot_hbm, cot_ref),
+            )
+        )
+    ]
+    for load in loads:
+        load.start()
+    for load in loads:
+        load.wait()
 
     def source_of(block):
         return edges_ref[0:1, block * LANES : (block + 1) * LANES]
@@ -181,11 +200,13 @@
                 copy(turn, k).start()
 
     def receive(turn):
-        for k in FACES + RIMS[::-1]:
-
-            @pl.when(there(k))
+        for rim, (faces, rims) in enumerate(counts):
+
+            @pl.when(at_rim == rim)
             def _():
-                copy(turn, 26 - k).wait_recv()
+                landed = ((face_in.at[turn, 0:faces], 0), (rim_in.at[turn, 0:rims], 1))
+                for block, which in landed:
+                    pltpu.make_async_copy(block, block, recv_sem.at[turn, which]).wait()
 
     def unpack(turn, codes):
         faces = face_in[turn].reshape(RIM_ROW, LANES)
@@ -230,108 +251,131 @@
             put_masked(block, pre * gate, target_of(block))
         return scatter(hot_target)
 
-    def edge_backward(layer, table):
-        deltas = []
+    def slope_sums(layer):
         for block in range(blocks):
-            delta = take(table, target_of(block)) * slopes[layer, :, block * LANES : (block + 1) * LANES]
-            deltas.append(delta)
-            put_masked(block, delta, target_of(block))
-        to_target = scatter(hot_target)
+            put_masked(block, slopes[layer, :, block * LANES : (block + 1) * LANES], target_of(block))
+        return scatter(hot_target)
+
+    def edge_backward(layer, table, summed):
         for block in range(blocks):
-            put_masked(block, deltas[block], source_of(block))
-        to_source = scatter(hot_source)
-        return jnp.concatenate([to_source, to_target], axis=0)
-
-    ends, joint, own, out, mixed = [], [], [], [], []
-    for layer in range(2):
-        entry = edge_in_ref[layer]
-        node = node_in_ref[layer]
-        ends.append(jnp.concatenate([entry[:, :F], entry[:, F:]], axis=0))
-        own.append(node[:, :F])
-        out.append(node_out_ref[layer])
-        wide = jnp.concatenate([edge_out_ref[layer]] * 4, axis=1)
-        mixed.append(times(spread(node[:, F:]), wide)[:, :F])
-
-    field = x_ref[...]
+            slope = slopes[layer, :, block * LANES : (block + 1) * LANES]
+            put_masked(block, take(table, target_of(block)) * slope, source_of(block))
+        return jnp.concatenate([scatter(hot_source), table * summed], axis=0)
+
+    def tiled(matrix):
+        return jnp.concatenate([matrix] * 4, axis=1)
+
+    own, out, mix, own_back, out_back, mix_back = [2 * at for at in range(6)]
+    entry = [jnp.concatenate([edge_in_ref[layer][:, :F], edge_in_ref[layer][:, F:]], axis=0) for layer in range(2)]
     build_hot(hot_target, target_of)
-    sums = edge_forward(0, times(spread(ends[0]), field))
+    sums = edge_forward(0, times(spread(entry[0]), x_ref[...]))
     pack(0, sums)
+    rim_counts = [f + r for f, r in counts]
+    present = jnp.int32(rim_counts[0])
+    for rim in range(1, 4):
+        present = jnp.where(at_rim == rim, rim_counts[rim], present)
     pl.semaphore_wait(barrier, present)
     send(0)
 
+    for layer in range(2):
+        node = node_in_ref[layer]
+        mixed = times(spread(node[:, F:]), tiled(edge_out_ref[layer]))[:, :F]
+        small_to[own + layer] = spread(node[:, :F])
+        small_to[out + layer] = spread(node_out_ref[layer])
+        small_to[mix + layer] = spread(mixed)
+        small_to[own_back + layer] = spread_flipped(node[:, :F])
+        small_to[out_back + layer] = spread_flipped(node_out_ref[layer])
+        small_to[mix_back + layer] = spread_flipped(mixed)
+        ends_from[layer] = spread_flipped(entry[layer])
+    ends_to[0] = spread(entry[1])
+    through = times(ends_to[0], tiled(node_out_ref[0]))[:, :F]
+    ends_to[1] = spread(through)
+    ends_from[2] = spread_flipped(through)
     codes = node_slots()
     build_hot(hot_source, source_of)
-    held[0] = times(spread(own[0]), field)
+    held[4] = slope_sums(0)
+    field = x_ref[...]
+    held[0] = times(small_to[own], field)
+    both_ends = times(ends_to[0], field)
+    held[5] = both_ends[:F]
+    held[6] = both_ends[F:]
     receive(0)
-    pre = held[0] + times(spread(mixed[0]), sums + unpack(0, codes))
+    pre = held[0] + times(small_to[mix], sums + unpack(0, codes))
     gate = sigmoid_of(pre)
-    node_slope = gate * (1.0 + pre * (1.0 - gate))
-    field = field + times(spread(out[0]), pre * gate)
-
-    sums = edge_forward(1, times(spread(ends[1]), field))
+    active = pre * gate
+    held[7] = gate * (1.0 + pre * (1.0 - gate))
+    table = jnp.concatenate([held[5], held[6]], axis=0) + times(ends_to[1], active)
+    sums = edge_forward(1, table)
     pack(1, sums)
     send(1)
-    held[1] = times(spread(own[1]), field)
-    cot = cot_ref[...]
-    lifted = times(spread_flipped(out[1]), cot)
+    field = field + times(small_to[out], active)
+    held[1] = times(small_to[own + 1], field)
+    held[8] = times(small_to[out_back + 1], cot_ref[...])
+    held[5] = slope_sums(1)
     receive(1)
-    pre = held[1] + times(spread(mixed[1]), sums + unpack(1, codes))
+    pre = held[1] + times(small_to[mix + 1], sums + unpack(1, codes))
     gate = sigmoid_of(pre)
 
-    delta = lifted * (gate * (1.0 + pre * (1.0 - gate)))
-    sums = times(spread_flipped(mixed[1]), delta)
+    delta = held[8] * (gate * (1.0 + pre * (1.0 - gate)))
+    sums = times(small_to[mix_back + 1], delta)
     pack(2, sums)
     send(2)
-    updated_ref[...] = field + times(spread(out[1]), pre * gate)
-    held[2] = cot + times(spread_flipped(own[1]), delta)
+    updated_ref[...] = field + times(small_to[out + 1], pre * gate)
+    held[2] = cot_ref[...] + times(small_to[own_back + 1], delta)
+    held[6] = times(small_to[out_back], held[2])
     receive(2)
-    both = edge_backward(1, sums + unpack(2, codes))
-    upstream = held[2] + times(spread_flipped(ends[1]), both)
-    delta = times(spread_flipped(out[0]), upstream) * node_slope
-    sums = times(spread_flipped(mixed[0]), delta)
+    both = edge_backward(1, sums + unpack(2, codes), held[5])
+    delta = (held[6] + times(ends_from[2], both)) * held[7]
+    sums = times(small_to[mix_back], delta)
     pack(3, sums)
     send(3)
-    held[3] = upstream + times(spread_flipped(own[0]), delta)
+    held[3] = held[2] + times(ends_from[1], both) + times(small_to[own_back], delta)
     receive(3)
-    both = edge_backward(0, sums + unpack(3, codes))
-    grad_ref[...] = held[3] + times(spread_flipped(ends[0]), both)
-
-    for turn in range(4):
-        for k in ORDER:
-
-            @pl.when(there(k))
-            def _():
-                copy(turn, k).wait_send()
+    both = edge_backward(0, sums + unpack(3, codes), held[4])
+    grad_ref[...] = held[3] + times(ends_from[0], both)
+
+    for rim, (faces, rims) in enumerate(counts):
+
+        @pl.when(at_rim == rim)
+        def _():
+            for block, which in ((face_out.at[:, 0:faces], 0), (rim_out.at[:, 0:rims], 1)):
+                pltpu.make_async_copy(block, block, send_sem.at[which]).wait()
 
 
 def solution(mesh):
     sizes = tuple(mesh.shape[axis] for axis in AXES)
 
-    def on_device(features, edge_lists, peer_nodes, edge_in, edge_out, node_in, node_out, cotangent):
-        nodes = features.shape[1]
-        edges = edge_lists.shape[1]
+    def on_device(*operands):
+        nodes = operands[0].shape[1]
+        edges = operands[1].shape[1]
+        anywhere = pl.BlockSpec(memory_space=pl.ANY)
         vmem = pl.BlockSpec(memory_space=pltpu.VMEM)
         return pl.pallas_call(
             functools.partial(kernel, sizes),
-            out_shape=(jax.ShapeDtypeStruct(features.shape, f32), jax.ShapeDtypeStruct(features.shape, f32)),
-            in_specs=[vmem] * 8,
+            out_shape=(jax.ShapeDtypeStruct((F, nodes), f32), jax.ShapeDtypeStruct((F, nodes), f32)),
+            in_specs=[anywhere] * len(operands),
             out_specs=(vmem, vmem),
             scratch_shapes=[
+                *(pltpu.VMEM(operand.shape, operand.dtype) for operand in operands),
+                pltpu.SemaphoreType.DMA((len(operands),)),
                 pltpu.VMEM((256, edges), bf16),
                 pltpu.VMEM((256, edges), bf16),
                 pltpu.VMEM((2, F, edges), f32),
                 pltpu.VMEM((128, edges), bf16),
                 pltpu.VMEM((LANES, LANES), i32),
-                pltpu.VMEM((4, F, nodes), f32),
+                pltpu.VMEM((9, F, nodes), f32),
+                pltpu.VMEM((2, 2 * F, LANES), bf16),
+                pltpu.VMEM((12, F, LANES), bf16),
+                pltpu.VMEM((3, F, 2 * LANES), bf16),
                 pltpu.VMEM((4, len(FACES), 8, LANES), f32),
                 pltpu.VMEM((4, 27, 1, LANES), f32),
                 pltpu.VMEM((4, len(FACES), 8, LANES), f32),
                 pltpu.VMEM((4, 27, 1, LANES), f32),
-                pltpu.SemaphoreType.DMA((4, 27)),
-                pltpu.SemaphoreType.DMA((4, 27)),
+                pltpu.SemaphoreType.DMA((2,)),
+                pltpu.SemaphoreType.DMA((4, 2)),
             ],
             compiler_params=pltpu.CompilerParams(collective_id=0, has_side_effects=True),
-        )(features, edge_lists, peer_nodes, edge_in, edge_out, node_in, node_out, cotangent)
+        )(*operands)
 
     split_columns = P(None, AXES)
     return jax.shard_map(

time: 40.5 us -> 38 us (0.938)
  Pallas kernels: 37.3 us -> 35 us
    pallas_call x1, Pallas kernels: 37.3 us -> 35 us  [on_device(): pl.pallas_call(functools.partial(kernel, sizes), out_shape=(jax.ShapeDtyp...]
where the time goes in v1:
time: 38 us; the launch traced here: 37.8 us
  Pallas kernels  35 us (92%)
  local copies, waits for them, and re-layouts  2.14 us (6%)
  between operations  0.65 us (2%)
    pallas_call x1, Pallas kernels, on_device(): pl.pallas_call(functools.partial(kernel, sizes), out_shape=(jax.ShapeDtyp...  35 us
    unnamed x4, local copies, waits for them, and re-layouts  2.14 us

profile of v1, /device:TPU:1, one launch (start us, length us, event | category | flops | bytes accessed | tf_op | source)
XLA Modules:
  0.0 37.8 jit_solution(687275256395083310)
XLA Ops:
  0.6 35.0 %shard_map.95 = (f32[32,512]{1,0:T(8,128)}, f32[32,512]{1,0:T(8,128)}) custom-call(f32[32,512]{1,0:T(8,128)} %x_hbm.1, s32[2,2048]{1,0:T(2,128)} %edges_hbm.1, s32[27,32]{1,0:T(8,128)} %peers_hbm.1, f32[2,32,64]{2,1,0:T(8,128)} %edge_in_hbm.1, f32[2,32,32]{2,1,0:T(8,128)} %edge_out_hbm.1, f32[2,32,64]{2,1,0:T(8,128)} %node_in_hbm.1, ...), custom_call_target="tpu_custom_call" | custom-call | tf_op jit(solution)/shard_map/pallas_call | solution.py:353
  35.7 0.0 copy-start
  35.7 1.5 %copy.12 = f32[32,512]{1,0:T(8,128)} copy(f32[32,512]{1,0:T(8,128)} %get-tuple-element.4) | data formatting | bytes 131072
  37.2 0.0 copy-done
  37.2 0.6 %copy.13 = f32[32,512]{1,0:T(8,128)} copy(f32[32,512]{1,0:T(8,128)S(1)} %copy-done) | data formatting | bytes 131072
Async XLA Ops:
  35.7 1.5 %copy-start = (f32[32,512]{1,0:T(8,128)S(1)}, f32[32,512]{1,0:T(8,128)}, u32[]{:S(2)}) copy-start(f32[32,512]{1,0:T(8,128)} %get-tuple-element.5) | copy-start | bytes 196612

commit v2 on v1

--- a/solution.py
+++ b/solution.py
@@ -17,6 +17,8 @@
 ORDER = sorted(RIMS, key=lambda k: -REACH[k]) + FACES
 RIM_ROW = 8 * len(FACES)
 ROWS = 80
+FORWARD_PRODUCTS = 16
+BACKWARD_PRODUCTS = 8
 f32, bf16, i32 = jnp.float32, jnp.bfloat16, jnp.int32
 
 
@@ -229,6 +231,8 @@
         return jnp.concatenate(pieces, axis=1)
 
     def put_masked(block, value, index):
+        if 2 * block >= blocks:
+            value = 0.5 * value
         half = jnp.broadcast_to(index >> 8, (F, LANES))
         columns = slice(block * LANES, (block + 1) * LANES)
         for part in range(2):
@@ -237,15 +241,37 @@
             masked[64 * part + 32 : 64 * part + 64, columns] = low
 
     def scatter(hot):
-        total = lax.dot_general(
-            masked[...], hot[...], (((1,), (1,)), ((), ())), preferred_element_type=f32
-        )
-        return jnp.concatenate([total[0:32] + total[32:64], total[64:96] + total[96:128]], axis=1)
+        first, second = [
+            lax.dot_general(
+                masked[:, columns], hot[:, columns], (((1,), (1,)), ((), ())), preferred_element_type=f32
+            )
+            for columns in (slice(0, edges // 2), slice(edges // 2, edges))
+        ]
+        total = [first[at : at + 32] + 2.0 * second[at : at + 32] for at in range(0, 128, 32)]
+        return jnp.concatenate([total[0] + total[1], total[2] + total[3]], axis=1)
+
+    def take_target(table, start, stop):
+        high, low = split(table)
+        left = jnp.concatenate([high[:, :256], low[:, :256], high[:, 256:], low[:, 256:]], axis=0)
+        pieces = []
+        for block in range(start, stop, 2):
+            width = min(2, stop - block)
+            got = dot(left, hot_target[:, block * LANES : (block + width) * LANES])
+            for at in range(width):
+                half = jnp.broadcast_to(target_of(block + at) >> 8, (F, LANES))
+                part = got[:, at * LANES : (at + 1) * LANES]
+                lower = jnp.where(half == 0, part[0:32] + part[32:64], 0.0)
+                pieces.append(jnp.where(half == 1, part[64:96] + part[96:128], lower))
+        return pieces
+
+    def by_target(table, products):
+        return take_target(table, 0, products) + [take(table, target_of(block)) for block in range(products, blocks)]
 
     def edge_forward(layer, table):
         first, second = table[:F], table[F:]
+        at_target = by_target(second, FORWARD_PRODUCTS)
         for block in range(blocks):
-            pre = take(first, source_of(block)) + take(second, target_of(block))
+            pre = take(first, source_of(block)) + at_target[block]
             gate = sigmoid_of(pre)
             slopes[layer, :, block * LANES : (block + 1) * LANES] = gate * (1.0 + pre * (1.0 - gate))
             put_masked(block, pre * gate, target_of(block))
@@ -257,9 +283,10 @@
         return scatter(hot_target)
 
     def edge_backward(layer, table, summed):
+        at_target = by_target(table, BACKWARD_PRODUCTS)
         for block in range(blocks):
             slope = slopes[layer, :, block * LANES : (block + 1) * LANES]
-            put_masked(block, take(table, target_of(block)) * slope, source_of(block))
+            put_masked(block, at_target[block] * slope, source_of(block))
         return jnp.concatenate([scatter(hot_source), table * summed], axis=0)
 
     def tiled(matrix):
@@ -352,7 +379,7 @@
         vmem = pl.BlockSpec(memory_space=pltpu.VMEM)
         return pl.pallas_call(
             functools.partial(kernel, sizes),
-            out_shape=(jax.ShapeDtypeStruct((F, nodes), f32), jax.ShapeDtypeStruct((F, nodes), f32)),
+            out_shape=(pltpu.VMEM((F, nodes), f32), pltpu.VMEM((F, nodes), f32)),
             in_specs=[anywhere] * len(operands),
             out_specs=(vmem, vmem),
             scratch_shapes=[

time: 38 us -> 35.1 us (0.924)
  Pallas kernels: 35 us -> 33 us
  local copies, waits for them, and re-layouts: 2.14 us -> 1.26 us
    pallas_call x1, Pallas kernels: 35 us -> 33 us  [on_device(): pl.pallas_call(functools.partial(kernel, sizes), out_shape=(pltpu.VMEM((F...]
    unnamed x4 -> x2, local copies, waits for them, and re-layouts: 2.14 us -> 1.26 us
where the time goes in v2:
time: 35.1 us; the launch traced here: 34.9 us
  Pallas kernels  33 us (94%)
  local copies, waits for them, and re-layouts  1.26 us (4%)
  between operations  0.64 us (2%)
    pallas_call x1, Pallas kernels, on_device(): pl.pallas_call(functools.partial(kernel, sizes), out_shape=(pltpu.VMEM((F...  33 us
    unnamed x2, local copies, waits for them, and re-layouts  1.26 us

profile of v2, /device:TPU:1, one launch (start us, length us, event | category | flops | bytes accessed | tf_op | source)
XLA Modules:
  0.0 34.9 jit_solution(1294488817337247395)
XLA Ops:
  0.6 33.0 %shard_map.95 = (f32[32,512]{1,0:T(8,128)S(1)}, f32[32,512]{1,0:T(8,128)S(1)}) custom-call(f32[32,512]{1,0:T(8,128)} %x_hbm.1, s32[2,2048]{1,0:T(2,128)} %edges_hbm.1, s32[27,32]{1,0:T(8,128)} %peers_hbm.1, f32[2,32,64]{2,1,0:T(8,128)} %edge_in_hbm.1, f32[2,32,32]{2,1,0:T(8,128)} %edge_out_hbm.1, f32[2,32,64]{2,1,0:T(8,128)} %node_in_hbm.1, ...), custom_call_target="tpu_custom_call" | custom-call | tf_op jit(solution)/shard_map/pallas_call | solution.py:380
  33.7 0.6 %copy.12 = f32[32,512]{1,0:T(8,128)} copy(f32[32,512]{1,0:T(8,128)S(1)} %get-tuple-element.2) | data formatting | bytes 131072
  34.3 0.6 %copy.13 = f32[32,512]{1,0:T(8,128)} copy(f32[32,512]{1,0:T(8,128)S(1)} %get-tuple-element.3) | data formatting | bytes 131072

commit v3 on v2

--- a/solution.py
+++ b/solution.py
@@ -17,6 +17,7 @@
 ORDER = sorted(RIMS, key=lambda k: -REACH[k]) + FACES
 RIM_ROW = 8 * len(FACES)
 ROWS = 80
+SOURCE_PRODUCTS = 6
 FORWARD_PRODUCTS = 16
 BACKWARD_PRODUCTS = 8
 f32, bf16, i32 = jnp.float32, jnp.bfloat16, jnp.int32
@@ -186,9 +187,12 @@
             codes.append(jnp.sum(code, axis=0, keepdims=True).astype(i32))
         return codes
 
-    def pack(turn, field):
-        columns = [take(field, slot_node[g : g + 1]) for g in range(4)]
-        packed = jnp.transpose(jnp.concatenate(columns, axis=0))
+    def at_slots(field):
+        return jnp.concatenate([take(field, slot_node[g : g + 1]) for g in range(4)], axis=1)
+
+    def ship(turn, columns):
+        tall = jnp.concatenate([columns[:, g * LANES : (g + 1) * LANES] for g in range(4)], axis=0)
+        packed = jnp.transpose(tall)
         for p in range(len(FACES)):
             face_out[turn, p] = packed[8 * p : 8 * p + 8]
         for k in RIMS:
@@ -210,12 +214,15 @@
                 for block, which in landed:
                     pltpu.make_async_copy(block, block, recv_sem.at[turn, which]).wait()
 
-    def unpack(turn, codes):
+    def arrivals(turn):
         faces = face_in[turn].reshape(RIM_ROW, LANES)
         rims = rim_in[turn].reshape(rim_in.shape[1], LANES)
         arrived = jnp.concatenate([faces, rims], axis=0)
         arrived = jnp.concatenate([arrived, jnp.zeros((LANES - arrived.shape[0], LANES), f32)], axis=0)
-        columns = jnp.transpose(arrived)
+        return jnp.transpose(arrived)
+
+    def unpack(turn, codes):
+        columns = arrivals(turn)
         pieces = []
         for chunk in range(chunks):
             code = jnp.broadcast_to(codes[chunk] - 1, (8, LANES))
@@ -250,28 +257,29 @@
         total = [first[at : at + 32] + 2.0 * second[at : at + 32] for at in range(0, 128, 32)]
         return jnp.concatenate([total[0] + total[1], total[2] + total[3]], axis=1)
 
-    def take_target(table, start, stop):
+    def take_products(table, hot, index_of, stop):
         high, low = split(table)
         left = jnp.concatenate([high[:, :256], low[:, :256], high[:, 256:], low[:, 256:]], axis=0)
         pieces = []
-        for block in range(start, stop, 2):
-            width = min(2, stop - block)
-            got = dot(left, hot_target[:, block * LANES : (block + width) * LANES])
-            for at in range(width):
-                half = jnp.broadcast_to(target_of(block + at) >> 8, (F, LANES))
+        for block in range(0, stop, 2):
+            got = dot(left, hot[:, block * LANES : (block + 2) * LANES])
+            for at in range(2):
+                half = jnp.broadcast_to(index_of(block + at) >> 8, (F, LANES))
                 part = got[:, at * LANES : (at + 1) * LANES]
                 lower = jnp.where(half == 0, part[0:32] + part[32:64], 0.0)
                 pieces.append(jnp.where(half == 1, part[64:96] + part[96:128], lower))
         return pieces
 
-    def by_target(table, products):
-        return take_target(table, 0, products) + [take(table, target_of(block)) for block in range(products, blocks)]
+    def at_ends(table, hot, index_of, products):
+        pieces = take_products(table, hot, index_of, products)
+        return pieces + [take(table, index_of(block)) for block in range(products, blocks)]
 
     def edge_forward(layer, table):
         first, second = table[:F], table[F:]
-        at_target = by_target(second, FORWARD_PRODUCTS)
+        at_target = at_ends(second, hot_target, target_of, FORWARD_PRODUCTS)
+        at_source = at_ends(first, hot_source, source_of, SOURCE_PRODUCTS if layer else 0)
         for block in range(blocks):
-            pre = take(first, source_of(block)) + at_target[block]
+            pre = at_source[block] + at_target[block]
             gate = sigmoid_of(pre)
             slopes[layer, :, block * LANES : (block + 1) * LANES] = gate * (1.0 + pre * (1.0 - gate))
             put_masked(block, pre * gate, target_of(block))
@@ -283,7 +291,7 @@
         return scatter(hot_target)
 
     def edge_backward(layer, table, summed):
-        at_target = by_target(table, BACKWARD_PRODUCTS)
+        at_target = at_ends(table, hot_target, target_of, BACKWARD_PRODUCTS)
         for block in range(blocks):
             slope = slopes[layer, :, block * LANES : (block + 1) * LANES]
             put_masked(block, at_target[block] * slope, source_of(block))
@@ -296,7 +304,7 @@
     entry = [jnp.concatenate([edge_in_ref[layer][:, :F], edge_in_ref[layer][:, F:]], axis=0) for layer in range(2)]
     build_hot(hot_target, target_of)
     sums = edge_forward(0, times(spread(entry[0]), x_ref[...]))
-    pack(0, sums)
+    ship(0, at_slots(sums))
     rim_counts = [f + r for f, r in counts]
     present = jnp.int32(rim_counts[0])
     for rim in range(1, 4):
@@ -333,20 +341,27 @@
     held[7] = gate * (1.0 + pre * (1.0 - gate))
     table = jnp.concatenate([held[5], held[6]], axis=0) + times(ends_to[1], active)
     sums = edge_forward(1, table)
-    pack(1, sums)
+    ship(1, at_slots(sums))
     send(1)
     field = field + times(small_to[out], active)
     held[1] = times(small_to[own + 1], field)
     held[8] = times(small_to[out_back + 1], cot_ref[...])
     held[5] = slope_sums(1)
+    local = held[1] + times(small_to[mix + 1], sums)
+    held[9] = at_slots(local)
+    held[10] = at_slots(held[8])
     receive(1)
+    arrived = arrivals(1)
+    arrived = jnp.concatenate([arrived[F * g : F * g + F] for g in range(4)], axis=1)
+    pre = held[9] + times(small_to[mix + 1], arrived)
+    gate = sigmoid_of(pre)
+    delta = held[10] * (gate * (1.0 + pre * (1.0 - gate)))
+    ship(2, times(small_to[mix_back + 1], delta))
+    send(2)
     pre = held[1] + times(small_to[mix + 1], sums + unpack(1, codes))
     gate = sigmoid_of(pre)
-
     delta = held[8] * (gate * (1.0 + pre * (1.0 - gate)))
     sums = times(small_to[mix_back + 1], delta)
-    pack(2, sums)
-    send(2)
     updated_ref[...] = field + times(small_to[out + 1], pre * gate)
     held[2] = cot_ref[...] + times(small_to[own_back + 1], delta)
     held[6] = times(small_to[out_back], held[2])
@@ -354,7 +369,7 @@
     both = edge_backward(1, sums + unpack(2, codes), held[5])
     delta = (held[6] + times(ends_from[2], both)) * held[7]
     sums = times(small_to[mix_back], delta)
-    pack(3, sums)
+    ship(3, at_slots(sums))
     send(3)
     held[3] = held[2] + times(ends_from[1], both) + times(small_to[own_back], delta)
     receive(3)
@@ -390,7 +405,7 @@
                 pltpu.VMEM((2, F, edges), f32),
                 pltpu.VMEM((128, edges), bf16),
                 pltpu.VMEM((LANES, LANES), i32),
-                pltpu.VMEM((9, F, nodes), f32),
+                pltpu.VMEM((11, F, nodes), f32),
                 pltpu.VMEM((2, 2 * F, LANES), bf16),
                 pltpu.VMEM((12, F, LANES), bf16),
                 pltpu.VMEM((3, F, 2 * LANES), bf16),

time: 35.1 us -> 34.5 us (0.983)
  Pallas kernels: 33 us -> 32.4 us
    pallas_call x1, Pallas kernels: 33 us -> 32.4 us  [on_device(): pl.pallas_call(functools.partial(kernel, sizes), out_shape=(pltpu.VMEM((F...]
where the time goes in v3:
time: 34.5 us; the launch traced here: 34.3 us
  Pallas kernels  32.4 us (94%)
  local copies, waits for them, and re-layouts  1.26 us (4%)
  between operations  0.64 us (2%)
    pallas_call x1, Pallas kernels, on_device(): pl.pallas_call(functools.partial(kernel, sizes), out_shape=(pltpu.VMEM((F...  32.4 us
    unnamed x2, local copies, waits for them, and re-layouts  1.26 us

profile of v3, /device:TPU:1, one launch (start us, length us, event | category | flops | bytes accessed | tf_op | source)
XLA Modules:
  0.0 34.3 jit_solution(8464805050532994013)
XLA Ops:
  0.6 32.4 %shard_map.95 = (f32[32,512]{1,0:T(8,128)S(1)}, f32[32,512]{1,0:T(8,128)S(1)}) custom-call(f32[32,512]{1,0:T(8,128)} %x_hbm.1, s32[2,2048]{1,0:T(2,128)} %edges_hbm.1, s32[27,32]{1,0:T(8,128)} %peers_hbm.1, f32[2,32,64]{2,1,0:T(8,128)} %edge_in_hbm.1, f32[2,32,32]{2,1,0:T(8,128)} %edge_out_hbm.1, f32[2,32,64]{2,1,0:T(8,128)} %node_in_hbm.1, ...), custom_call_target="tpu_custom_call" | custom-call | tf_op jit(solution)/shard_map/pallas_call | solution.py:395
  33.1 0.6 %copy.12 = f32[32,512]{1,0:T(8,128)} copy(f32[32,512]{1,0:T(8,128)S(1)} %get-tuple-element.2) | data formatting | bytes 131072
  33.7 0.6 %copy.13 = f32[32,512]{1,0:T(8,128)} copy(f32[32,512]{1,0:T(8,128)S(1)} %get-tuple-element.3) | data formatting | bytes 131072

commit v4 on v3

--- a/solution.py
+++ b/solution.py
@@ -392,7 +392,7 @@
         edges = operands[1].shape[1]
         anywhere = pl.BlockSpec(memory_space=pl.ANY)
         vmem = pl.BlockSpec(memory_space=pltpu.VMEM)
-        return pl.pallas_call(
+        results = pl.pallas_call(
             functools.partial(kernel, sizes),
             out_shape=(pltpu.VMEM((F, nodes), f32), pltpu.VMEM((F, nodes), f32)),
             in_specs=[anywhere] * len(operands),
@@ -419,6 +419,24 @@
             compiler_params=pltpu.CompilerParams(collective_id=0, has_side_effects=True),
         )(*operands)
 
+        def store(updated_ref, grad_ref, updated_out, grad_out, sems):
+            copies = [
+                pltpu.make_async_copy(updated_ref, updated_out, sems.at[0]),
+                pltpu.make_async_copy(grad_ref, grad_out, sems.at[1]),
+            ]
+            for copy in copies:
+                copy.start()
+            for copy in copies:
+                copy.wait()
+
+        return pl.pallas_call(
+            store,
+            out_shape=(jax.ShapeDtypeStruct((F, nodes), f32), jax.ShapeDtypeStruct((F, nodes), f32)),
+            in_specs=[vmem, vmem],
+            out_specs=(anywhere, anywhere),
+            scratch_shapes=[pltpu.SemaphoreType.DMA((2,))],
+        )(*[pltpu.with_memory_space_constraint(result, pltpu.VMEM) for result in results])
+
     split_columns = P(None, AXES)
     return jax.shard_map(
         on_device,

time: 34.5 us -> 33.9 us (0.983)
  local copies, waits for them, and re-layouts: 1.26 us -> 0 us
  Pallas kernels: 32.4 us -> 33.1 us
    unnamed x2 -> x0, local copies, waits for them, and re-layouts: 1.26 us -> none
    pallas_call x0 -> x1, Pallas kernels: none -> 0.67 us  [on_device(): pl.pallas_call(store, out_shape=(jax.ShapeDtypeStruct((F, nodes), f32), j...]
where the time goes in v4:
time: 33.9 us; the launch traced here: 33.7 us
  Pallas kernels  33.1 us (98%)
  between operations  0.64 us (2%)
    pallas_call x1, Pallas kernels, on_device(): pl.pallas_call(functools.partial(kernel, sizes), out_shape=(pltpu.VMEM((F...  32.4 us

profile of v4, /device:TPU:1, one launch (start us, length us, event | category | flops | bytes accessed | tf_op | source)
XLA Modules:
  0.0 33.7 jit_solution(17713896993830790837)
XLA Ops:
  0.6 32.4 %shard_map.95 = (f32[32,512]{1,0:T(8,128)S(1)}, f32[32,512]{1,0:T(8,128)S(1)}) custom-call(f32[32,512]{1,0:T(8,128)} %x_hbm.1, s32[2,2048]{1,0:T(2,128)} %edges_hbm.1, s32[27,32]{1,0:T(8,128)} %peers_hbm.1, f32[2,32,64]{2,1,0:T(8,128)} %edge_in_hbm.1, f32[2,32,32]{2,1,0:T(8,128)} %edge_out_hbm.1, f32[2,32,64]{2,1,0:T(8,128)} %node_in_hbm.1, ...), custom_call_target="tpu_custom_call" | custom-call | tf_op jit(solution)/shard_map/pallas_call | solution.py:395
  33.1 0.7 %shard_map.96 = (f32[32,512]{1,0:T(8,128)}, f32[32,512]{1,0:T(8,128)}) custom-call(f32[32,512]{1,0:T(8,128)S(1)} %get-tuple-element.4.updated_ref, f32[32,512]{1,0:T(8,128)S(1)} %get-tuple-element.5.grad_ref), custom_call_target="tpu_custom_call" | custom-call | tf_op jit(solution)/shard_map/pallas_call | solution.py:432
